TPU v7x, 32 devices: a whole 2x2x4 slice. The times are simulated.
32 devices in a mesh: fsdp: 4 (over z), tp: 4 (over y, core), sect: 2 (over x).
Axes of the slice: x: 2, y: 2, z: 4, core: 2. Of those that a mesh axis runs over, the one named last changes fastest.
Arguments:
- hidden: bfloat16 [4096, 8192], P('fsdp', 'sect'), may hold values from -6 to 6
- kv_weight: bfloat16 [8192, 2048], P(('sect', 'fsdp'), 'tp'), may hold values from -0.0625 to 0.0625
- readout: float32 [2048], P(('tp', 'sect')), may hold values from -0.125 to 0.125
- lengths: int32 [4, 4], P('fsdp'), may hold values from 1 to 512, as said below
- prompt_mask: int32 [4096], P('fsdp'), may hold values from 0 to 1, as said below
- group_ids: int32 [16], P('fsdp'), may hold values from 0 to 1
Outputs:
- keys_values: bfloat16 [4096, 2048], P('fsdp', ('tp', 'sect'))
- advantages: float32 [16], P('fsdp')
Inputs may be any that keep to these rules, and one draw needn't show every extreme that they name: `lengths`: each row sums to 1024; some entry of each row equals 512. `prompt_mask`: within each sequence the zeros come before the ones; at each index of fsdp exactly one sequence has no ones.
All inputs are finite; a program needn't handle non-finite values.
Results may differ from a plain program's by a relative error of at most 0.00045.
Values may be sent and summed in bfloat16 or wider, within the bound.
A program may use at most 64 MiB of HBM per device.

v0:
```python
import jax
import jax.numpy as jnp
from jax import lax
from jax.sharding import PartitionSpec as P


def swapped(value, axis, bit):
    mask = 2**bit
    pairs = [(source, source ^ mask) for source in range(lax.axis_size(axis))]
    return lax.ppermute(value, axis, pairs)


def local(hidden, kv_weight, readout, lengths, prompt_mask, group_ids):
    block_width = kv_weight.shape[1]
    col_width = block_width // lax.axis_size("sect")
    sect_index = lax.axis_index("sect")
    tok_rows = hidden.shape[0]

    def add_rows(piece):
        return jnp.dot(hidden, piece, preferred_element_type=jnp.float32)

    partner_cols = lax.dynamic_slice_in_dim(kv_weight, (1 - sect_index) * col_width, col_width, 1)
    partner_part = add_rows(lax.all_gather(partner_cols, "fsdp", axis=0, tiled=True))
    received = swapped(partner_part, "sect", 0)
    own_cols = lax.dynamic_slice_in_dim(kv_weight, sect_index * col_width, col_width, 1)
    own_part = add_rows(lax.all_gather(own_cols, "fsdp", axis=0, tiled=True))
    projected = own_part + received
    keys_values = projected.astype(jnp.bfloat16)
    partial_score = jnp.dot(projected, readout, precision=lax.Precision.HIGHEST)
    token_score = lax.psum(partial_score, ("tp", "sect"))
    mask_float = prompt_mask.astype(jnp.float32)
    row_len = lengths[0]
    finish = jnp.cumsum(row_len)
    starts = finish - row_len
    places = jnp.arange(tok_rows, dtype=jnp.int32)
    member = ((places[None, :] >= starts[:, None]) & (places[None, :] < finish[:, None])).astype(
        jnp.float32
    )
    seq_sum = jnp.dot(member, token_score * mask_float, precision=lax.Precision.HIGHEST)
    count = jnp.dot(member, mask_float, precision=lax.Precision.HIGHEST)
    reward = seq_sum / jnp.sqrt(jnp.maximum(count, 1.0))
    group_count = group_ids.shape[0] * lax.axis_size("fsdp") // 8
    onehot = (group_ids[:, None] == jnp.arange(group_count, dtype=jnp.int32)[None, :]).astype(
        jnp.float32
    )
    local_sizes = jnp.sum(onehot, axis=0)
    local_sums = jnp.sum(onehot * reward[:, None], axis=0)
    group_sums, group_sizes = lax.psum((local_sums, local_sizes), "fsdp")
    mean_g = group_sums / jnp.maximum(group_sizes, 1.0)
    own_mean = jnp.sum(onehot * mean_g[None, :], axis=1)
    local_dev = jnp.sum(onehot * ((reward - own_mean) ** 2)[:, None], axis=0)
    spread = lax.psum(local_dev, "fsdp")
    var_g = spread / jnp.maximum(group_sizes, 1.0)
    own_var = jnp.sum(onehot * var_g[None, :], axis=1)
    advantages = (reward - own_mean) / jnp.sqrt(own_var + 1.0)
    return (keys_values, advantages)


def solution(mesh):
    return jax.shard_map(
        local,
        mesh=mesh,
        in_specs=(
            P("fsdp", "sect"),
            P(("sect", "fsdp"), "tp"),
            P(("tp", "sect")),
            P("fsdp", None),
            P("fsdp"),
            P("fsdp"),
        ),
        out_specs=(P("fsdp", ("tp", "sect")), P("fsdp")),
        check_vma=False,
    )
```

profile of v0, /device:TPU:0, one launch (start us, length us, event | category | flops | bytes accessed | tf_op | source)
XLA Modules:
  0.0 153.3 jit_solution(12628619160099686405)
XLA Ops:
  7.2 0.0 copy-start
  7.2 0.0 all-gather.5.cloned.1.call-start
  7.2 2.2 %constant_dynamic-slice_fusion.1 = (bf16[1024,256]{1,0:T(8,128)(2,1)}, bf16[1024,256]{1,0:T(8,128)(2,1)}) fusion(bf16[1024,512]{1,0:T(8,128)(2,1)} %param.7, s32[]{:T(128)S(6)} %select_n.6, s32[]{:T(128)S(6)} %select_n.7), kind=kLoop, calls=%fused_computation.20 | loop fusion | bytes 2097160 | tf_op jit(solution)/shard_map/dynamic_slice | solution.py:25
  9.5 0.0 all-gather.5.cloned.1.call-update
  9.5 0.0 all-gather.3.cloned.1.call-start
  9.5 0.7 all-gather.3.cloned.1.call-update
  10.2 0.0 copy-start.3
  10.3 0.0 copy-start.1
  10.3 47.8 %all-gather.5.cloned.1.call-done = bf16[4096,256]{1,0:T(8,128)(2,1)} async-done(((bf16[1024,256]{1,0:T(8,128)(2,1)}), bf16[4096,256]{1,0:T(8,128)(2,1)}) %all-gather.5.cloned.1.call-update) | async-done | bytes 2097168 | tf_op jit(solution)/shard_map/all_gather | solution.py:23
  58.0 6.4 %convolution_bitcast_fusion = f32[1024,256]{0,1:T(8,128)S(1)} fusion(bf16[4096,256]{1,0:T(8,128)(2,1)} %all-gather.5.cloned.1.call-done, bf16[1024,4096]{1,0:T(8,128)(2,1)} %param.6), kind=kOutput, calls=%fused_computation | convolution fusion | flops 2147483648 | bytes 11534336 | tf_op jit(solution)/shard_map/dot_general | solution.py:20
  64.4 1.5 collective-permute-start
  66.0 0.0 copy-done.3
  66.0 0.2 reduce-window.7
  66.1 0.0 copy-done.1
  66.2 0.0 copy-start.2
  66.2 38.5 %all-gather.3.cloned.1.call-done = bf16[4096,256]{1,0:T(8,128)(2,1)} async-done(((bf16[1024,256]{1,0:T(8,128)(2,1)}), bf16[4096,256]{1,0:T(8,128)(2,1)}) %all-gather.3.cloned.1.call-update) | async-done | bytes 2097168 | tf_op jit(solution)/shard_map/all_gather | solution.py:26
  104.7 0.0 collective-permute-done
  104.7 6.4 %fusion.8 = (bf16[1024,256]{0,1:T(8,128)(2,1)S(1)}, f32[1024,256]{0,1:T(8,128)S(1)}) fusion(f32[1024,256]{0,1:T(8,128)S(1)} %collective-permute-done, bf16[4096,256]{1,0:T(8,128)(2,1)} %all-gather.3.cloned.1.call-done, bf16[1024,4096]{1,0:T(8,128)(2,1)} %param.6), kind=kOutput, calls=%fused_computation.25 | convolution fusion | flops 2148007936 | bytes 13107200 | tf_op jit(solution)/shard_map/dot_general | solution.py:20
  111.1 0.0 copy-done
  111.1 0.6 fusion.9
  111.8 13.5 %psum.28 = f32[1024]{0:T(1024)S(1)} all-reduce(f32[1024]{0:T(1024)S(1)} %bitcast.34), channel_id=1, replica_groups=mesh['fsdp'=4,'tp'=4,'sect'=2] {'tp','sect'}, use_global_device_ids=true, to_apply=%region_1.0 | all-reduce | flops 1024 | bytes 8192 | tf_op jit(solution)/shard_map/psum | solution.py:30
  125.3 0.2 convolution_bitcast_fusion.3
  125.5 0.2 fusion.3
  125.7 0.0 copy-done.2
  125.7 0.2 convert_reduce_fusion
  125.9 9.8 %all-reduce = (f32[2]{0:T(128)S(1)}, f32[2]{0:T(128)S(1)}) all-reduce(f32[2]{0:T(128)S(1)} %get-tuple-element.7, f32[2]{0:T(128)S(1)} %get-tuple-element.6), channel_id=1, replica_groups=mesh['fsdp'=4,'tp'=4,'sect'=2] {'fsdp'}, use_global_device_ids=true, to_apply=%region_3.4 | all-reduce | flops 4 | bytes 32 | tf_op jit(solution)/shard_map/psum | solution.py:48
  135.7 0.1 select_reduce_fusion.2
  135.8 0.1 select_reduce_fusion.1
  135.9 8.9 %psum.31 = f32[2]{0:T(128)S(1)} all-reduce(f32[2]{0:T(128)S(1)} %select_reduce_fusion.1), channel_id=1, replica_groups=mesh['fsdp'=4,'tp'=4,'sect'=2] {'fsdp'}, use_global_device_ids=true, to_apply=%region_8.9 | all-reduce | flops 2 | bytes 16 | tf_op jit(solution)/shard_map/psum | solution.py:52
  144.9 0.1 select_reduce_fusion
  145.0 1.0 copy.9
  146.0 0.5 rsqrt_multiply_fusion
  (6 shorter events, 0.0 us)
Async XLA Ops:
  7.2 104.0 %copy-start = (f32[256]{0:T(256)S(1)}, f32[256]{0:T(256)}, u32[]{:S(2)}) copy-start(f32[256]{0:T(256)} %param.8) | copy-start | bytes 3076
  7.2 50.9 %all-gather.5.cloned.1.call-start = ((), (), s32[]{:S(2)}) async-start(), calls=%async_computation.1 | async-start | bytes 2621440 | tf_op jit(solution)/shard_map/all_gather | solution.py:23
  9.5 95.2 %all-gather.3.cloned.1.call-start = ((), (), s32[]{:S(2)}) async-start(), calls=%async_computation | async-start | bytes 2621440 | tf_op jit(solution)/shard_map/all_gather | solution.py:26
  10.2 55.7 %copy-start.3 = (s32[1,4]{1,0:T(1,128)S(1)}, s32[1,4]{1,0:T(1,128)}, u32[]{:S(2)}) copy-start(s32[1,4]{1,0:T(1,128)} %param.9) | copy-start | bytes 52
  10.3 55.9 %copy-start.1 = (s32[1024]{0:T(1024)S(1)}, s32[1024]{0:T(1024)}, u32[]{:S(2)}) copy-start(s32[1024]{0:T(1024)} %param.10) | copy-start | bytes 12292
  64.4 40.3 %collective-permute-start = (f32[1024,256]{0,1:T(8,128)S(1)}, f32[1024,256]{0,1:T(8,128)S(1)}, u32[]{:S(2)}, u32[]{:S(2)}) collective-permute-start(f32[1024,256]{0,1:T(8,128)S(1)} %convolution_bitcast_fusion), channel_id=1, source_target_pairs={{0,1},{1,0},{2,3},{3,2},{4,5},{5,4},{6,7},{7,6},{8,9},{9,8},{10,11... | collective-permute-start | bytes 3145736 | tf_op jit(solution)/shard_map/ppermute | solution.py:10
  66.2 59.6 %copy-start.2 = (s32[4]{0:T(128)S(1)}, s32[4]{0:T(128)}, u32[]{:S(2)}) copy-start(s32[4]{0:T(128)} %param.11) | copy-start | bytes 52
Sparse Core Ops, SparseCore 0:
  9.6 48.3 all-gather.4
  60.2 44.4 all-gather.2
where the time goes:
time: 154 us; the launch traced here: 153 us
  waiting for transfers between devices  87 us (56%)
  blocking collectives  32.3 us (21%)
  between operations  14.1 us (9%)
  matrix products  13.9 us (9%)
  local copies, waits for them, and re-layouts  3.28 us (2%)
  starting transfers between devices  1.61 us (1%)
    all_gather x1, waiting for transfers between devices, local(): lax.all_gather(partner_cols, 'fsdp', axis=0, tiled=True)  47.8 us
    all_gather x1, waiting for transfers between devices, local(): own_part = add_rows(lax.all_gather(own_cols, 'fsdp', axis=0, tiled=True))  38.5 us
    psum x1, blocking collectives, local(): token_score = lax.psum(partial_score, ('tp', 'sect'))  13.5 us
    dot_general x2, matrix products, add_rows(): return jnp.dot(hidden, piece, preferred_element_type=jnp.float32)  12.8 us
    psum x1, blocking collectives, local(): group_sums, group_sizes = lax.psum((local_sums, local_sizes), 'fsdp')  9.81 us
    psum x1, blocking collectives, local(): spread = lax.psum(local_dev, 'fsdp')  8.94 us
  transfers between devices with their start and end apart: 3, of which 2 were waited for; matrix products, arithmetic and copies ran while one was open for 4% of the time, Pallas kernels for 0%

commit v1 on v0

v1 whole, which is shorter than its diff:
```python
import functools

import jax
import jax.numpy as jnp
from jax import lax
from jax.experimental import pallas as pl
from jax.experimental.pallas import tpu as pltpu
from jax.sharding import PartitionSpec as P

MESH = pl.DeviceIdType.MESH


def kernel(
    n, nt, ns, chunks, tile,
    hid_any, w_any, ro_ref, mask_ref, len_ref, gid_ref,
    kv_any, adv_ref,
    hid, wbuf, psend, precv, kvbuf, member, sbuf, zbuf,
    hid_sem, own_sem, kv_sem, wsend, wrecv, xsend, xrecv, ssend, srecv, zsend, zrecv,
):
    f, t, s = lax.axis_index("fsdp"), lax.axis_index("tp"), lax.axis_index("sect")
    plane = nt * ns
    me = t * ns + s
    rows, width = w_any.shape
    cw = width // chunks
    half = chunks // 2
    tok = hid.shape[0]

    def plane_id(k):
        other = lax.rem(me + k, plane)
        return {"tp": lax.div(other, ns), "sect": lax.rem(other, ns)}

    def line_id(k):
        return {"fsdp": lax.rem(f + k, n)}

    def cols(c):
        start = lax.rem(c * cw + (1 - s) * (width // 2), width)
        return pl.ds(pl.multiple_of(start, cw), cw)

    def block(c, j):
        return wbuf.at[c, pl.ds(pl.multiple_of(j * rows, rows), rows), :]

    def w_copy(c, j, step, own):
        return pltpu.make_async_remote_copy(
            src_ref=w_any.at[:, cols(c)] if own else block(c, j),
            dst_ref=block(c, j),
            send_sem=wsend.at[0 if step > 0 else 1, c, j],
            recv_sem=wrecv.at[c, j],
            device_id={"fsdp": f + step},
            device_id_type=MESH,
        )

    def x_copy(c):
        return pltpu.make_async_remote_copy(
            src_ref=psend.at[c],
            dst_ref=precv.at[c],
            send_sem=xsend.at[c],
            recv_sem=xrecv.at[c],
            device_id={"sect": 1 - s},
            device_id_type=MESH,
        )

    def s_copy(k, slot):
        return pltpu.make_async_remote_copy(
            src_ref=sbuf.at[slot],
            dst_ref=sbuf.at[slot],
            send_sem=ssend.at[k],
            recv_sem=srecv.at[slot],
            device_id=plane_id(k),
            device_id_type=MESH,
        )

    def z_copy(k, slot):
        return pltpu.make_async_remote_copy(
            src_ref=zbuf.at[slot],
            dst_ref=zbuf.at[slot],
            send_sem=zsend.at[k],
            recv_sem=zrecv.at[slot],
            device_id=line_id(k),
            device_id_type=MESH,
        )

    def each(low, high, body):
        def step(i, carry):
            body(i)
            return carry

        lax.fori_loop(low, high, step, 0)

    barrier = pltpu.get_barrier_semaphore()
    each(1, n, lambda k: pl.semaphore_signal(
        barrier, inc=1, device_id=line_id(k), device_id_type=MESH))
    each(1, plane, lambda k: pl.semaphore_signal(
        barrier, inc=1, device_id=plane_id(k), device_id_type=MESH))

    def own_copy(c):
        return pltpu.make_async_copy(w_any.at[:, cols(c)], block(c, f), own_sem.at[c])

    pl.semaphore_wait(barrier, n - 1 + plane - 1)

    for c in range(chunks):
        @pl.when(f < n - 1)
        def _():
            w_copy(c, f, 1, True).start()

        @pl.when(f > 0)
        def _():
            w_copy(c, f, -1, True).start()

    hid_copy = pltpu.make_async_copy(hid_any, hid, hid_sem)
    for c in range(chunks):
        own_copy(c).start()
    hid_copy.start()

    place = lax.broadcasted_iota(jnp.int32, (8, tok), 1)
    seq = lax.broadcasted_iota(jnp.int32, (8, tok), 0)
    inside = jnp.zeros((8, tok), jnp.bool_)
    start = jnp.int32(0)
    n_seq = len_ref.shape[1]
    for j in range(n_seq):
        finish = start + len_ref[0, j]
        inside = inside | ((seq == j) & (place >= start) & (place < finish))
        start = finish
    member[...] = inside.astype(jnp.float32) * mask_ref[...].astype(jnp.float32)

    total = jnp.zeros((8, cw), jnp.float32)
    for c in range(chunks):
        def arrive(d, c=c):
            left, right = f - d, f + d

            @pl.when(left >= 0)
            def _():
                w_copy(c, left, -1, False).wait_recv()

                @pl.when(f < n - 1)
                def _():
                    w_copy(c, left, 1, False).start()

            @pl.when(right < n)
            def _():
                w_copy(c, right, 1, False).wait_recv()

                @pl.when(f > 0)
                def _():
                    w_copy(c, right, -1, False).start()

        each(1, n, arrive)
        own_copy(c).wait()
        if c == 0:
            hid_copy.wait()
        if c >= half:
            x_copy(c - half).wait_recv()
        own = c - half

        def product(i, carry, c=c, own=own):
            at = pl.ds(pl.multiple_of(i * tile, tile), tile)
            part = jnp.dot(hid[at, :], wbuf[c], preferred_element_type=jnp.float32)
            if c < half:
                psend[c, at, :] = part
                return carry
            projected = part + precv[own, at, :]
            kvbuf[at, own * cw:(own + 1) * cw] = projected.astype(jnp.bfloat16)
            picked = jnp.dot(
                member[:, at], projected,
                precision=lax.Precision.HIGHEST, preferred_element_type=jnp.float32,
            )
            return carry + picked * ro_ref[:, own * cw:(own + 1) * cw]

        total = lax.fori_loop(0, tok // tile, product, total)
        if c < half:
            x_copy(c).start()

    kv_copy = pltpu.make_async_copy(kvbuf, kv_any, kv_sem)
    kv_copy.start()
    sbuf[me] = total
    each(1, plane, lambda k: s_copy(k, me).start())
    count = jnp.sum(member[...], axis=1, keepdims=True)
    each(1, plane, lambda k: s_copy(k, lax.rem(me + k, plane)).wait_recv())
    seq_sum = jnp.sum(jnp.sum(sbuf[...], axis=0), axis=1, keepdims=True)
    reward = seq_sum / jnp.sqrt(jnp.maximum(count, 1.0))

    row = lax.broadcasted_iota(jnp.int32, (8, 128), 0)
    lane = lax.broadcasted_iota(jnp.int32, (8, 128), 1)
    row_gid = jnp.full((8, 128), -1, jnp.int32)
    lane_gid = jnp.full((8, 128), -2, jnp.int32)
    for j in range(n_seq):
        row_gid = jnp.where(row == j, gid_ref[j], row_gid)
        lane_gid = jnp.where(lane == j, gid_ref[j], lane_gid)
    reward = jnp.broadcast_to(reward, (8, 128))
    zbuf[f, 0] = reward
    zbuf[f, 1] = row_gid.astype(jnp.float32)
    each(1, n, lambda k: z_copy(k, f).start())
    mine = jnp.sum(jnp.where(row == lane, reward, 0.0), axis=0, keepdims=True)
    each(1, n, lambda k: z_copy(k, lax.rem(f + k, n)).wait_recv())
    same = (zbuf[:, 1] == lane_gid.astype(jnp.float32)[None]).astype(jnp.float32)
    rewards = zbuf[:, 0]

    def over(value):
        return jnp.sum(jnp.sum(value, axis=0), axis=0, keepdims=True)

    size = jnp.maximum(over(same), 1.0)
    mean = over(same * rewards) / size
    var = over(same * (rewards - mean[None]) ** 2) / size
    adv_ref[...] = ((mine - mean) / jnp.sqrt(var + 1.0))[:, :n_seq]

    each(1, plane, lambda k: s_copy(k, me).wait_send())
    each(1, n, lambda k: z_copy(k, f).wait_send())
    for c in range(half):
        x_copy(c).wait_send()
    for c in range(chunks):
        def sent(j, c=c):
            @pl.when((j <= f) & (f < n - 1))
            def _():
                w_copy(c, j, 1, False).wait_send()

            @pl.when((j >= f) & (f > 0))
            def _():
                w_copy(c, j, -1, False).wait_send()

        each(0, n, sent)
    kv_copy.wait()


def solution(mesh):
    n, nt, ns = mesh.shape["fsdp"], mesh.shape["tp"], mesh.shape["sect"]

    def local(hidden, kv_weight, readout, lengths, prompt_mask, group_ids):
        tok, depth = hidden.shape
        rows, width = kv_weight.shape
        chunks = 4 if n <= 16 else 2
        cw = width // chunks
        half = chunks // 2
        plane = nt * ns
        n_seq = lengths.shape[1]
        dma = pltpu.SemaphoreType.DMA
        vmem, smem, anywhere = (
            pl.BlockSpec(memory_space=pltpu.VMEM),
            pl.BlockSpec(memory_space=pltpu.SMEM),
            pl.BlockSpec(memory_space=pl.ANY),
        )
        kv, adv = pl.pallas_call(
            functools.partial(kernel, n, nt, ns, chunks, min(256, tok)),
            out_shape=(
                jax.ShapeDtypeStruct((tok, width // 2), jnp.bfloat16),
                jax.ShapeDtypeStruct((1, n_seq), jnp.float32),
            ),
            in_specs=[anywhere, anywhere, vmem, vmem, smem, smem],
            out_specs=(anywhere, vmem),
            scratch_shapes=[
                pltpu.VMEM((tok, depth), jnp.bfloat16),
                pltpu.VMEM((chunks, depth, cw), jnp.bfloat16),
                pltpu.VMEM((half, tok, cw), jnp.float32),
                pltpu.VMEM((half, tok, cw), jnp.float32),
                pltpu.VMEM((tok, width // 2), jnp.bfloat16),
                pltpu.VMEM((8, tok), jnp.float32),
                pltpu.VMEM((plane, 8, cw), jnp.float32),
                pltpu.VMEM((n, 2, 8, 128), jnp.float32),
                dma, dma((chunks,)), dma,
                dma((2, chunks, n)), dma((chunks, n)),
                dma((half,)), dma((half,)),
                dma((plane,)), dma((plane,)),
                dma((n,)), dma((n,)),
            ],
            compiler_params=pltpu.CompilerParams(collective_id=0, has_side_effects=True),
        )(hidden, kv_weight, readout[None, :], prompt_mask[None, :], lengths, group_ids)
        return kv, adv[0]

    return jax.shard_map(
        local,
        mesh=mesh,
        in_specs=(
            P("fsdp", "sect"),
            P(("sect", "fsdp"), "tp"),
            P(("tp", "sect")),
            P("fsdp", None),
            P("fsdp"),
            P("fsdp"),
        ),
        out_specs=(P("fsdp", ("tp", "sect")), P("fsdp")),
        check_vma=False,
    )
```

time: 154 us -> 92 us (0.60)
  Pallas kernels: 0 us -> 88.2 us
  waiting for transfers between devices: 87 us -> 0 us
  blocking collectives: 32.3 us -> 0 us
  matrix products: 13.9 us -> 0 us
  between operations: 14.1 us -> 0.64 us
  starting transfers between devices: 1.61 us -> 0 us
    pallas_call x0 -> x1, Pallas kernels: none -> 88.2 us  [local(): pl.pallas_call(functools.partial(kernel, n, nt, ns, chunks, min(256, tok)...]
    all_gather x2 -> x0, waiting for transfers between devices: 86.3 us -> none  [the longest x1 47.8 us: local(): lax.all_gather(partner_cols, 'fsdp', axis=0, tiled=True)]
    psum x3 -> x0, blocking collectives: 32.3 us -> none  [the longest x1 13.5 us: local(): token_score = lax.psum(partial_score, ('tp', 'sect'))]
    dot_general x5 -> x0, matrix products: 13.9 us -> none  [the longest x2 12.8 us: add_rows(): return jnp.dot(hidden, piece, preferred_element_type=jnp.float32)]
    dynamic_slice x1 -> x0, local copies, waits for them, and re-layouts: 2.24 us -> none  [local(): lax.dynamic_slice_in_dim(kv_weight, sect_index * col_width, col_width, 1)]
    unnamed x9 -> x2, local copies, waits for them, and re-layouts: 1.04 us -> 2.97 us
  transfers between devices with their start and end apart: 3 -> 0, of which waited for: 2 -> 0; matrix products, arithmetic and copies ran while one was open for 4% -> 0% of each run, Pallas kernels for 0% -> 0%
where the time goes in v1:
time: 92 us; the launch traced here: 91.8 us
  Pallas kernels  88.2 us (96%)
  local copies, waits for them, and re-layouts  2.97 us (3%)
    pallas_call x1, Pallas kernels, local(): pl.pallas_call(functools.partial(kernel, n, nt, ns, chunks, min(256, tok)...  88.2 us
    unnamed x2, local copies, waits for them, and re-layouts  2.97 us

profile of v1, /device:TPU:0, one launch (start us, length us, event | category | flops | bytes accessed | tf_op | source)
XLA Modules:
  0.0 91.8 jit_solution(308900070790103181)
XLA Ops:
  0.6 88.2 %shard_map.77 = (bf16[1024,256]{1,0:T(8,128)(2,1)}, f32[1,4]{1,0:T(1,128)}) custom-call(bf16[1024,4096]{1,0:T(8,128)(2,1)} %hid_any.1, bf16[1024,512]{1,0:T(8,128)(2,1)} %w_any.1, f32[1,256]{1,0:T(1,128)} %bitcast.4, s32[1,1024]{1,0:T(1,128)} %bitcast.3, s32[1,4]{1,0:T(1,128)} %len_ref.1, s32[4]{0:T(128)} %gid_ref.1), custom_call_target="tpu_custom_call" | custom-call | tf_op jit(solution)/shard_map/pallas_call | solution.py:240
  88.9 1.9 %copy.10 = bf16[1024,256]{1,0:T(8,128)(2,1)} copy(bf16[1024,256]{1,0:T(8,128)(2,1)} %get-tuple-element.8) | data formatting | bytes 1048576
  90.7 1.1 %copy.11 = f32[4]{0:T(128)} copy(f32[4]{0:T(128)} %bitcast.5) | data formatting | bytes 32

commit v2 on v1

v2 whole, which is shorter than its diff:
```python
import functools

import jax
import jax.numpy as jnp
from jax import lax
from jax.experimental import pallas as pl
from jax.experimental.pallas import tpu as pltpu
from jax.sharding import PartitionSpec as P

MESH = pl.DeviceIdType.MESH


def kernel(
    n, nt, ns, parts, tile,
    hid_any, w_any, ro_ref, mask_ref, len_ref, gid_ref,
    kv_ref, adv_ref,
    hid, wbuf, acc, precv, member, sbuf, zbuf,
    hid_sem, own_sem, wsend, wrecv, xsend, xrecv, ssend, srecv, zsend, zrecv,
):
    f, t, s = lax.axis_index("fsdp"), lax.axis_index("tp"), lax.axis_index("sect")
    plane = nt * ns
    me = t * ns + s
    rows, width = w_any.shape
    cw = width // 2
    piece = rows // parts
    by_piece = piece % 128 == 0
    tok = hid.shape[0]

    def plane_id(k):
        other = lax.rem(me + k, plane)
        return {"tp": lax.div(other, ns), "sect": lax.rem(other, ns)}

    def line_id(k):
        return {"fsdp": lax.rem(f + k, n)}

    def cols(c):
        side = s if c else 1 - s
        return pl.ds(pl.multiple_of(side * cw, cw), cw)

    def depth_at(j, r):
        return pl.ds(pl.multiple_of(j * rows + r * piece, piece), piece)

    def own_rows(c, r):
        return w_any.at[r * piece:(r + 1) * piece, cols(c)]

    def w_copy(c, j, r, step, own):
        place = wbuf.at[c, depth_at(j, r), :]
        return pltpu.make_async_remote_copy(
            src_ref=own_rows(c, r) if own else place,
            dst_ref=place,
            send_sem=wsend.at[0 if step > 0 else 1, c, r, j],
            recv_sem=wrecv.at[c, r, j],
            device_id={"fsdp": f + step},
            device_id_type=MESH,
        )

    def x_copy():
        return pltpu.make_async_remote_copy(
            src_ref=acc.at[0],
            dst_ref=precv,
            send_sem=xsend,
            recv_sem=xrecv,
            device_id={"sect": 1 - s},
            device_id_type=MESH,
        )

    def s_copy(k, slot):
        return pltpu.make_async_remote_copy(
            src_ref=sbuf.at[slot],
            dst_ref=sbuf.at[slot],
            send_sem=ssend.at[k],
            recv_sem=srecv.at[slot],
            device_id=plane_id(k),
            device_id_type=MESH,
        )

    def z_copy(k, slot):
        return pltpu.make_async_remote_copy(
            src_ref=zbuf.at[slot],
            dst_ref=zbuf.at[slot],
            send_sem=zsend.at[k],
            recv_sem=zrecv.at[slot],
            device_id=line_id(k),
            device_id_type=MESH,
        )

    def each(low, high, body):
        def step(i, carry):
            body(i)
            return carry

        lax.fori_loop(low, high, step, 0)

    barrier = pltpu.get_barrier_semaphore()
    each(1, n, lambda k: pl.semaphore_signal(
        barrier, inc=1, device_id=line_id(k), device_id_type=MESH))
    each(1, plane, lambda k: pl.semaphore_signal(
        barrier, inc=1, device_id=plane_id(k), device_id_type=MESH))

    def own_copy(c, r):
        return pltpu.make_async_copy(
            own_rows(c, r), wbuf.at[c, depth_at(f, r), :], own_sem.at[c, r])

    def send_own(c, step):
        for r in range(parts):
            w_copy(c, f, r, step, True).start()

    pl.semaphore_wait(barrier, n - 1 + plane - 1)

    @pl.when(f < n - 1)
    def _():
        send_own(0, 1)

    @pl.when(f > 0)
    def _():
        send_own(0, -1)

    @pl.when(f == 0)
    def _():
        send_own(1, 1)

    @pl.when(f == n - 1)
    def _():
        send_own(1, -1)

    hid_copy = pltpu.make_async_copy(hid_any, hid, hid_sem)
    for c in range(2):
        for r in range(parts):
            own_copy(c, r).start()
    hid_copy.start()

    place = lax.broadcasted_iota(jnp.int32, (8, tok), 1)
    seq = lax.broadcasted_iota(jnp.int32, (8, tok), 0)
    inside = jnp.zeros((8, tok), jnp.bool_)
    start = jnp.int32(0)
    n_seq = len_ref.shape[1]
    for j in range(n_seq):
        finish = start + len_ref[0, j]
        inside = inside | ((seq == j) & (place >= start) & (place < finish))
        start = finish
    member[...] = inside.astype(jnp.float32) * mask_ref[...].astype(jnp.float32)

    def add(c, depth, first):
        def product(i, carry):
            at = pl.ds(pl.multiple_of(i * tile, tile), tile)
            part = jnp.dot(
                hid[at, depth], wbuf[c, depth, :], preferred_element_type=jnp.float32)
            acc[c, at, :] = part if first else acc[c, at, :] + part
            return carry

        lax.fori_loop(0, tok // tile, product, 0)

    def arrive(c, j, r, step):
        w_copy(c, j, r, -step, False).wait_recv()

        @pl.when((f + step >= 0) & (f + step < n))
        def _():
            w_copy(c, j, r, step, False).start()

        if by_piece:
            add(c, depth_at(j, r), False)

    for c in range(2):
        for r in range(parts):
            own_copy(c, r).wait()
        if c == 0:
            hid_copy.wait()
        if by_piece:
            add(c, pl.ds(pl.multiple_of(f * rows, rows), rows), True)

        def visit(d, c=c):
            left, right = f - d, f + d
            for r in range(parts):
                @pl.when(left >= 0)
                def _():
                    arrive(c, left, r, 1)

                @pl.when(right < n)
                def _():
                    arrive(c, right, r, -1)

            if c == 0:
                @pl.when((d == f) & (f < n - 1))
                def _():
                    send_own(1, 1)

                @pl.when((d == n - 1 - f) & (f > 0))
                def _():
                    send_own(1, -1)

        each(1, n, visit)
        if not by_piece:
            add(c, slice(None), True)
        if c == 0:
            x_copy().start()

    x_copy().wait_recv()

    def finish_rows(i, carry):
        at = pl.ds(pl.multiple_of(i * tile, tile), tile)
        projected = acc[1, at, :] + precv[at, :]
        kv_ref[at, :] = projected.astype(jnp.bfloat16)
        return carry + jnp.dot(
            member[:, at], projected,
            precision=lax.Precision.HIGHEST, preferred_element_type=jnp.float32,
        )

    total = lax.fori_loop(
        0, tok // tile, finish_rows, jnp.zeros((8, cw), jnp.float32)) * ro_ref[...]
    sbuf[me] = total
    each(1, plane, lambda k: s_copy(k, me).start())
    count = jnp.sum(member[...], axis=1, keepdims=True)
    each(1, plane, lambda k: s_copy(k, lax.rem(me + k, plane)).wait_recv())
    seq_sum = jnp.sum(jnp.sum(sbuf[...], axis=0), axis=1, keepdims=True)
    reward = seq_sum / jnp.sqrt(jnp.maximum(count, 1.0))

    row = lax.broadcasted_iota(jnp.int32, (8, 128), 0)
    lane = lax.broadcasted_iota(jnp.int32, (8, 128), 1)
    row_gid = jnp.full((8, 128), -1, jnp.int32)
    lane_gid = jnp.full((8, 128), -2, jnp.int32)
    for j in range(n_seq):
        row_gid = jnp.where(row == j, gid_ref[j], row_gid)
        lane_gid = jnp.where(lane == j, gid_ref[j], lane_gid)
    reward = jnp.broadcast_to(reward, (8, 128))
    zbuf[f, 0] = reward
    zbuf[f, 1] = row_gid.astype(jnp.float32)
    each(1, n, lambda k: z_copy(k, f).start())
    mine = jnp.sum(jnp.where(row == lane, reward, 0.0), axis=0, keepdims=True)
    each(1, n, lambda k: z_copy(k, lax.rem(f + k, n)).wait_recv())
    same = (zbuf[:, 1] == lane_gid.astype(jnp.float32)[None]).astype(jnp.float32)
    rewards = zbuf[:, 0]

    def over(value):
        return jnp.sum(jnp.sum(value, axis=0), axis=0, keepdims=True)

    size = jnp.maximum(over(same), 1.0)
    mean = over(same * rewards) / size
    var = over(same * (rewards - mean[None]) ** 2) / size
    adv_ref[...] = ((mine - mean) / jnp.sqrt(var + 1.0))[:, :n_seq]

    each(1, plane, lambda k: s_copy(k, me).wait_send())
    each(1, n, lambda k: z_copy(k, f).wait_send())
    x_copy().wait_send()
    for c in range(2):
        def sent(j, c=c):
            for r in range(parts):
                @pl.when((j <= f) & (f < n - 1))
                def _():
                    w_copy(c, j, r, 1, False).wait_send()

                @pl.when((j >= f) & (f > 0))
                def _():
                    w_copy(c, j, r, -1, False).wait_send()

        each(0, n, sent)


def solution(mesh):
    n, nt, ns = mesh.shape["fsdp"], mesh.shape["tp"], mesh.shape["sect"]

    def local(hidden, kv_weight, readout, lengths, prompt_mask, group_ids):
        tok, depth = hidden.shape
        rows, width = kv_weight.shape
        parts = max(1, min(2, rows // 256))
        cw = width // 2
        plane = nt * ns
        n_seq = lengths.shape[1]
        dma = pltpu.SemaphoreType.DMA
        vmem, smem, anywhere = (
            pl.BlockSpec(memory_space=pltpu.VMEM),
            pl.BlockSpec(memory_space=pltpu.SMEM),
            pl.BlockSpec(memory_space=pl.ANY),
        )
        kv, adv = pl.pallas_call(
            functools.partial(kernel, n, nt, ns, parts, min(256, tok)),
            out_shape=(
                jax.ShapeDtypeStruct((tok, width // 2), jnp.bfloat16),
                jax.ShapeDtypeStruct((1, n_seq), jnp.float32),
            ),
            in_specs=[anywhere, anywhere, vmem, vmem, smem, smem],
            out_specs=(vmem, vmem),
            scratch_shapes=[
                pltpu.VMEM((tok, depth), jnp.bfloat16),
                pltpu.VMEM((2, depth, cw), jnp.bfloat16),
                pltpu.VMEM((2, tok, cw), jnp.float32),
                pltpu.VMEM((tok, cw), jnp.float32),
                pltpu.VMEM((8, tok), jnp.float32),
                pltpu.VMEM((plane, 8, cw), jnp.float32),
                pltpu.VMEM((n, 2, 8, 128), jnp.float32),
                dma, dma((2, parts)),
                dma((2, 2, parts, n)), dma((2, parts, n)),
                dma, dma,
                dma((plane,)), dma((plane,)),
                dma((n,)), dma((n,)),
            ],
            compiler_params=pltpu.CompilerParams(collective_id=0, has_side_effects=True),
        )(hidden, kv_weight, readout[None, :], prompt_mask[None, :], lengths, group_ids)
        return kv, adv[0]

    return jax.shard_map(
        local,
        mesh=mesh,
        in_specs=(
            P("fsdp", "sect"),
            P(("sect", "fsdp"), "tp"),
            P(("tp", "sect")),
            P("fsdp", None),
            P("fsdp"),
            P("fsdp"),
        ),
        out_specs=(P("fsdp", ("tp", "sect")), P("fsdp")),
        check_vma=False,
    )
```

time: 92 us -> 89.5 us (0.973)
  Pallas kernels: 88.2 us -> 85.7 us
    pallas_call x1, Pallas kernels: 88.2 us -> 85.7 us  [local(): pl.pallas_call(functools.partial(kernel, n, nt, ns, parts, min(256, tok))...]
where the time goes in v2:
time: 89.5 us; the launch traced here: 89.3 us
  Pallas kernels  85.7 us (96%)
  local copies, waits for them, and re-layouts  2.97 us (3%)
    pallas_call x1, Pallas kernels, local(): pl.pallas_call(functools.partial(kernel, n, nt, ns, parts, min(256, tok))...  85.7 us
    unnamed x2, local copies, waits for them, and re-layouts  2.97 us

profile of v2, /device:TPU:0, one launch (start us, length us, event | category | flops | bytes accessed | tf_op | source)
XLA Modules:
  0.0 89.3 jit_solution(5497878850963995652)
XLA Ops:
  0.6 85.7 %shard_map.77 = (bf16[1024,256]{1,0:T(8,128)(2,1)}, f32[1,4]{1,0:T(1,128)}) custom-call(bf16[1024,4096]{1,0:T(8,128)(2,1)} %hid_any.1, bf16[1024,512]{1,0:T(8,128)(2,1)} %w_any.1, f32[1,256]{1,0:T(1,128)} %bitcast.4, s32[1,1024]{1,0:T(1,128)} %bitcast.3, s32[1,4]{1,0:T(1,128)} %len_ref.1, s32[4]{0:T(128)} %gid_ref.1), custom_call_target="tpu_custom_call" | custom-call | tf_op jit(solution)/shard_map/pallas_call | solution.py:274
  86.3 1.9 %copy.10 = bf16[1024,256]{1,0:T(8,128)(2,1)} copy(bf16[1024,256]{1,0:T(8,128)(2,1)} %get-tuple-element.8) | data formatting | bytes 1048576
  88.2 1.1 %copy.11 = f32[4]{0:T(128)} copy(f32[4]{0:T(128)} %bitcast.5) | data formatting | bytes 32

commit v3 on v2

--- a/solution.py
+++ b/solution.py
@@ -253,6 +253,27 @@
                     w_copy(c, j, r, -1, False).wait_send()
 
         each(0, n, sent)
+
+
+def hand_over(pieces, kv_any, adv_in, kv_out, adv_out, held, in_sem, out_sem):
+    size = held.shape[1]
+
+    def load(i):
+        return pltpu.make_async_copy(
+            kv_any.at[i * size:(i + 1) * size], held.at[i], in_sem.at[i])
+
+    def store(i):
+        return pltpu.make_async_copy(
+            held.at[i], kv_out.at[i * size:(i + 1) * size], out_sem.at[i])
+
+    for i in range(pieces):
+        load(i).start()
+    adv_out[...] = adv_in[...]
+    for i in range(pieces):
+        load(i).wait()
+        store(i).start()
+    for i in range(pieces):
+        store(i).wait()
 
 
 def solution(mesh):
@@ -295,6 +316,21 @@
             ],
             compiler_params=pltpu.CompilerParams(collective_id=0, has_side_effects=True),
         )(hidden, kv_weight, readout[None, :], prompt_mask[None, :], lengths, group_ids)
+        pieces = 4 if tok % 64 == 0 else 1
+        kv, adv = pl.pallas_call(
+            functools.partial(hand_over, pieces),
+            out_shape=(
+                jax.ShapeDtypeStruct((tok, width // 2), jnp.bfloat16),
+                jax.ShapeDtypeStruct((1, n_seq), jnp.float32),
+            ),
+            in_specs=[anywhere, vmem],
+            out_specs=(anywhere, vmem),
+            scratch_shapes=[
+                pltpu.VMEM((pieces, tok // pieces, width // 2), jnp.bfloat16),
+                dma((pieces,)),
+                dma((pieces,)),
+            ],
+        )(kv, adv)
         return kv, adv[0]
 
     return jax.shard_map(

time: 89.5 us -> 89.5 us (level)
  Pallas kernels: 85.7 us -> 88.7 us
  local copies, waits for them, and re-layouts: 2.97 us -> 0 us
    pallas_call x0 -> x1, Pallas kernels: none -> 3 us  [local(): pl.pallas_call(functools.partial(hand_over, pieces), out_shape=(jax.Shape...]
    unnamed x2 -> x0, local copies, waits for them, and re-layouts: 2.97 us -> none
where the time goes in v3:
time: 89.5 us; the launch traced here: 89.3 us
  Pallas kernels  88.7 us (99%)
    pallas_call x1, Pallas kernels, local(): pl.pallas_call(functools.partial(kernel, n, nt, ns, parts, min(256, tok))...  85.7 us
    pallas_call x1, Pallas kernels, local(): pl.pallas_call(functools.partial(hand_over, pieces), out_shape=(jax.Shape...  3 us

profile of v3, /device:TPU:0, one launch (start us, length us, event | category | flops | bytes accessed | tf_op | source)
XLA Modules:
  0.0 89.3 jit_solution(16715841921930692075)
XLA Ops:
  0.6 85.7 %shard_map.77 = (bf16[1024,256]{1,0:T(8,128)(2,1)}, f32[1,4]{1,0:T(1,128)}) custom-call(bf16[1024,4096]{1,0:T(8,128)(2,1)} %hid_any.1, bf16[1024,512]{1,0:T(8,128)(2,1)} %w_any.1, f32[1,256]{1,0:T(1,128)} %bitcast.4, s32[1,1024]{1,0:T(1,128)} %bitcast.3, s32[1,4]{1,0:T(1,128)} %len_ref.1, s32[4]{0:T(128)} %gid_ref.1), custom_call_target="tpu_custom_call" | custom-call | tf_op jit(solution)/shard_map/pallas_call | solution.py:295
  86.3 3.0 %shard_map.78 = (bf16[1024,256]{1,0:T(8,128)(2,1)}, f32[1,4]{1,0:T(1,128)}) custom-call(bf16[1024,256]{1,0:T(8,128)(2,1)} %get-tuple-element.6.kv_any, f32[1,4]{1,0:T(1,128)} %get-tuple-element.7.adv_in), custom_call_target="tpu_custom_call" | custom-call | tf_op jit(solution)/shard_map/pallas_call | solution.py:320

commit v4 on v2

--- a/solution.py
+++ b/solution.py
@@ -274,8 +274,8 @@
         kv, adv = pl.pallas_call(
             functools.partial(kernel, n, nt, ns, parts, min(256, tok)),
             out_shape=(
-                jax.ShapeDtypeStruct((tok, width // 2), jnp.bfloat16),
-                jax.ShapeDtypeStruct((1, n_seq), jnp.float32),
+                pltpu.VMEM((tok, width // 2), jnp.bfloat16),
+                pltpu.VMEM((1, n_seq), jnp.float32),
             ),
             in_specs=[anywhere, anywhere, vmem, vmem, smem, smem],
             out_specs=(vmem, vmem),

time: 89.5 us -> 87 us (0.972)
  local copies, waits for them, and re-layouts: 2.97 us -> 1.31 us
    unnamed x2, local copies, waits for them, and re-layouts: 2.97 us -> 1.31 us
where the time goes in v4:
time: 87 us; the launch traced here: 86.8 us
  Pallas kernels  84.9 us (98%)
  local copies, waits for them, and re-layouts  1.31 us (2%)
    pallas_call x1, Pallas kernels, local(): pl.pallas_call(functools.partial(kernel, n, nt, ns, parts, min(256, tok))...  84.9 us

profile of v4, /device:TPU:0, one launch (start us, length us, event | category | flops | bytes accessed | tf_op | source)
XLA Modules:
  0.0 86.8 jit_solution(15738786244315310706)
XLA Ops:
  0.6 84.9 %shard_map.77 = (bf16[1024,256]{1,0:T(8,128)(2,1)S(1)}, f32[1,4]{1,0:T(1,128)S(1)}) custom-call(bf16[1024,4096]{1,0:T(8,128)(2,1)} %hid_any.1, bf16[1024,512]{1,0:T(8,128)(2,1)} %w_any.1, f32[1,256]{1,0:T(1,128)} %bitcast.5, s32[1,1024]{1,0:T(1,128)} %bitcast.4, s32[1,4]{1,0:T(1,128)} %len_ref.1, s32[4]{0:T(128)} %gid_ref.1), custom_call_target="tpu_custom_call" | custom-call | tf_op jit(solution)/shard_map/pallas_call | solution.py:274
  85.5 0.8 copy.10
  86.3 0.5 copy.11

commit v5 on v4

--- a/solution.py
+++ b/solution.py
@@ -207,7 +207,7 @@
 
     total = lax.fori_loop(
         0, tok // tile, finish_rows, jnp.zeros((8, cw), jnp.float32)) * ro_ref[...]
-    sbuf[me] = total
+    sbuf[me] = sum(total[:, at:at + 128] for at in range(0, cw, 128))
     each(1, plane, lambda k: s_copy(k, me).start())
     count = jnp.sum(member[...], axis=1, keepdims=True)
     each(1, plane, lambda k: s_copy(k, lax.rem(me + k, plane)).wait_recv())
@@ -261,7 +261,7 @@
     def local(hidden, kv_weight, readout, lengths, prompt_mask, group_ids):
         tok, depth = hidden.shape
         rows, width = kv_weight.shape
-        parts = max(1, min(2, rows // 256))
+        parts = max(1, min(4, rows // 256))
         cw = width // 2
         plane = nt * ns
         n_seq = lengths.shape[1]
@@ -285,7 +285,7 @@
                 pltpu.VMEM((2, tok, cw), jnp.float32),
                 pltpu.VMEM((tok, cw), jnp.float32),
                 pltpu.VMEM((8, tok), jnp.float32),
-                pltpu.VMEM((plane, 8, cw), jnp.float32),
+                pltpu.VMEM((plane, 8, 128), jnp.float32),
                 pltpu.VMEM((n, 2, 8, 128), jnp.float32),
                 dma, dma((2, parts)),
                 dma((2, 2, parts, n)), dma((2, parts, n)),

time: 87 us -> 87.3 us (level)
  no operation moved by 1% of the time
where the time goes in v5:
time: 87.3 us; the launch traced here: 87.1 us
  Pallas kernels  85.1 us (97%)
  local copies, waits for them, and re-layouts  1.31 us (2%)
    pallas_call x1, Pallas kernels, local(): pl.pallas_call(functools.partial(kernel, n, nt, ns, parts, min(256, tok))...  85.1 us

profile of v5, /device:TPU:0, one launch (start us, length us, event | category | flops | bytes accessed | tf_op | source)
XLA Modules:
  0.0 87.1 jit_solution(6949745704563642819)
XLA Ops:
  0.6 85.1 %shard_map.77 = (bf16[1024,256]{1,0:T(8,128)(2,1)S(1)}, f32[1,4]{1,0:T(1,128)S(1)}) custom-call(bf16[1024,4096]{1,0:T(8,128)(2,1)} %hid_any.1, bf16[1024,512]{1,0:T(8,128)(2,1)} %w_any.1, f32[1,256]{1,0:T(1,128)} %bitcast.5, s32[1,1024]{1,0:T(1,128)} %bitcast.4, s32[1,4]{1,0:T(1,128)} %len_ref.1, s32[4]{0:T(128)} %gid_ref.1), custom_call_target="tpu_custom_call" | custom-call | tf_op jit(solution)/shard_map/pallas_call | solution.py:274
  85.8 0.8 copy.10
  86.6 0.5 copy.11

commit v6 on v4

--- a/solution.py
+++ b/solution.py
@@ -200,10 +200,13 @@
         at = pl.ds(pl.multiple_of(i * tile, tile), tile)
         projected = acc[1, at, :] + precv[at, :]
         kv_ref[at, :] = projected.astype(jnp.bfloat16)
-        return carry + jnp.dot(
-            member[:, at], projected,
-            precision=lax.Precision.HIGHEST, preferred_element_type=jnp.float32,
-        )
+        chosen = member[:, at].astype(jnp.bfloat16)
+        rest = projected
+        for _ in range(3):
+            digits = rest.astype(jnp.bfloat16)
+            carry += jnp.dot(chosen, digits, preferred_element_type=jnp.float32)
+            rest = rest - digits.astype(jnp.float32)
+        return carry
 
     total = lax.fori_loop(
         0, tok // tile, finish_rows, jnp.zeros((8, cw), jnp.float32)) * ro_ref[...]

time: 87 us -> 86.9 us (level)
  no operation moved by 1% of the time
where the time goes in v6:
time: 86.9 us; the launch traced here: 86.7 us
  Pallas kernels  84.8 us (98%)
  local copies, waits for them, and re-layouts  1.31 us (2%)
    pallas_call x1, Pallas kernels, local(): pl.pallas_call(functools.partial(kernel, n, nt, ns, parts, min(256, tok))...  84.8 us

profile of v6, /device:TPU:0, one launch (start us, length us, event | category | flops | bytes accessed | tf_op | source)
XLA Modules:
  0.0 86.7 jit_solution(10991666208309042142)
XLA Ops:
  0.6 84.8 %shard_map.77 = (bf16[1024,256]{1,0:T(8,128)(2,1)S(1)}, f32[1,4]{1,0:T(1,128)S(1)}) custom-call(bf16[1024,4096]{1,0:T(8,128)(2,1)} %hid_any.1, bf16[1024,512]{1,0:T(8,128)(2,1)} %w_any.1, f32[1,256]{1,0:T(1,128)} %bitcast.5, s32[1,1024]{1,0:T(1,128)} %bitcast.4, s32[1,4]{1,0:T(1,128)} %len_ref.1, s32[4]{0:T(128)} %gid_ref.1), custom_call_target="tpu_custom_call" | custom-call | tf_op jit(solution)/shard_map/pallas_call | solution.py:277
  85.4 0.8 copy.10
  86.2 0.5 copy.11
